TPU v7x, 256 devices: a whole 4x4x8 slice. The times are simulated.
256 devices in a mesh: out: 32 (over x, z_hi, core), in: 8 (over z_lo, y).
Axes of the slice: x: 4, y: 4, z: 8 (z_hi: 4, z_lo: 2; z = z_hi * 2 + z_lo), core: 2. Of those that a mesh axis runs over, the one named last changes fastest.
Arguments:
- slopes: bfloat16 [256, 163840], P('out', 'in'), may hold values from -6 to 6
- cols_first: int32 [128, 64], P(None, 'in'), may hold values from 0 to 79
- count_first: int32 [128, 8], P('out', 'in'), may hold values from 1 to 8
- weight_first: bfloat16 [128, 64, 256, 256], P('out', 'in'), may hold values from -0.0625 to 0.0625
- bias_first: float32 [32768], P(('out', 'in')), may hold values from -3 to 3
- cols_second: int32 [128, 32], P('out', 'in'), may hold values from 0 to 15
- count_second: int32 [128, 8], P('out', 'in'), may hold values from 1 to 4
- weight_second: bfloat16 [128, 32, 256, 256], P('out', 'in'), may hold values from -0.09375 to 0.09375
- bias_second: float32 [32768], P(('out', 'in')), may hold values from -3 to 3
- cotangent: bfloat16 [256, 32768], P(None, ('out', 'in')), may hold values from -6 to 6
Outputs:
- estimate: bfloat16 [256, 32768], P(None, ('out', 'in'))
- grad_first: bfloat16 [128, 64, 256, 256], P('out', 'in')
- grad_second: bfloat16 [128, 32, 256, 256], P('out', 'in')
Inputs may be any that keep to these rules, and one draw needn't show every extreme that they name: `cols_first`: A local block index within the range of slopes of the slot's in index. `count_first`: slots of a block row at or after this count, within one in range, are not used. `cols_second`: A local block index within the range of reordered hidden units of the slot's in index. `count_second`: slots of a block row at or after this count, within one in range, are not used.
All inputs are finite; a program needn't handle non-finite values.
Results may differ from a plain program's by a relative error of at most 0.025.
Values may be sent and summed in bfloat16 or wider, within the bound.
No kernel may reach another device: no remote copies, remote signals or barrier semaphores. Data moves between devices by JAX's collectives and lax.ppermute only.
A program may use at most 128 MiB of HBM per device.

v0:
```python
import jax
import jax.numpy as jnp
from jax import lax
from jax.sharding import PartitionSpec as P

BLK = 256
KD1 = 8
KD2 = 4


def shards(
    slopes,
    cols_first,
    count_first,
    weight_first,
    bias_first,
    cols_second,
    count_second,
    weight_second,
    bias_second,
    cotangent,
):
    rows = weight_first.shape[0]
    live_first = jnp.arange(KD1, dtype=jnp.int32)[None, :] < count_first
    live_second = jnp.arange(KD2, dtype=jnp.int32)[None, :] < count_second
    masked_first = weight_first * live_first.astype(jnp.bfloat16)[:, :, None, None]
    masked_second = weight_second * live_second.astype(jnp.bfloat16)[:, :, None, None]
    gathered = lax.all_gather(slopes, "out", axis=0, tiled=True)
    frames = gathered.shape[0]
    slope_blocks = gathered.reshape(frames, -1, BLK)
    own_cols = lax.dynamic_slice_in_dim(cols_first, lax.axis_index("out") * rows, rows, 0)
    panels_first = jnp.take(slope_blocks, own_cols.reshape(-1), axis=1).reshape(
        frames, rows, KD1, BLK
    )
    partial_first = jnp.einsum(
        "frkb,rkbo->fro", panels_first, masked_first, preferred_element_type=jnp.float32
    ).reshape(frames, rows * BLK)
    summed_first = lax.psum_scatter(partial_first, "in", scatter_dimension=1, tiled=True)
    hidden_first = jnp.tanh(summed_first + bias_first[None, :]).astype(jnp.bfloat16)
    second_input = lax.all_gather(hidden_first, "out", axis=1, tiled=True)
    hidden_blocks = second_input.reshape(frames, -1, BLK)
    panels_second = jnp.take(hidden_blocks, cols_second.reshape(-1), axis=1).reshape(
        frames, rows, KD2, BLK
    )
    partial_second = jnp.einsum(
        "frkb,rkbo->fro", panels_second, masked_second, preferred_element_type=jnp.float32
    ).reshape(frames, rows * BLK)
    summed_second = lax.psum_scatter(partial_second, "in", scatter_dimension=1, tiled=True)
    estimate = jnp.tanh(summed_second + bias_second[None, :]).astype(jnp.bfloat16)
    est32 = estimate.astype(jnp.float32)
    delta_second = (cotangent.astype(jnp.float32) * (1.0 - est32 * est32)).astype(jnp.bfloat16)
    rows_second = lax.all_gather(delta_second, "in", axis=1, tiled=True).reshape(frames, rows, BLK)
    grad_second = jnp.einsum(
        "frkb,fro->rkbo", panels_second, rows_second, preferred_element_type=jnp.float32
    )
    grad_second = (grad_second * live_second.astype(jnp.float32)[:, :, None, None]).astype(
        jnp.bfloat16
    )
    adjoint = jnp.einsum(
        "fro,rkbo->frkb", rows_second, masked_second, preferred_element_type=jnp.float32
    ).reshape(frames, rows * KD2, BLK)
    selector = (
        cols_second.reshape(-1)[:, None]
        == jnp.arange(hidden_blocks.shape[1], dtype=jnp.int32)[None, :]
    ).astype(jnp.float32)
    spread = jnp.einsum("fjb,jc->fcb", adjoint, selector, precision=lax.Precision.HIGHEST).reshape(
        frames, -1
    )
    back_first = lax.psum_scatter(
        spread.astype(jnp.bfloat16), "out", scatter_dimension=1, tiled=True
    ).astype(jnp.float32)
    hid32 = hidden_first.astype(jnp.float32)
    delta_first = (back_first * (1.0 - hid32 * hid32)).astype(jnp.bfloat16)
    rows_first = lax.all_gather(delta_first, "in", axis=1, tiled=True).reshape(frames, rows, BLK)
    grad_first = jnp.einsum(
        "frkb,fro->rkbo", panels_first, rows_first, preferred_element_type=jnp.float32
    )
    grad_first = (grad_first * live_first.astype(jnp.float32)[:, :, None, None]).astype(
        jnp.bfloat16
    )
    return (estimate, grad_first, grad_second)


def solution(mesh):
    return jax.shard_map(
        shards,
        mesh=mesh,
        in_specs=(
            P("out", "in"),
            P(None, "in"),
            P("out", "in"),
            P("out", "in", None, None),
            P(("out", "in")),
            P("out", "in"),
            P("out", "in"),
            P("out", "in", None, None),
            P(("out", "in")),
            P(None, ("out", "in")),
        ),
        out_specs=(P(None, ("out", "in")), P("out", "in", None, None), P("out", "in", None, None)),
        check_vma=False,
    )
```

profile of v0, /device:TPU:24, one launch (start us, length us, event | category | flops | bytes accessed | tf_op | source)
XLA Modules:
  0.0 476.3 jit_solution(1294169107600888628)
XLA Ops:
  9.7 93.1 %all-gather.3.cloned.1.call-done = bf16[256,20480]{1,0:T(8,128)(2,1)} async-done(((bf16[8,20480]{1,0:T(8,128)(2,1)}), bf16[256,20480]{1,0:T(8,128)(2,1)}) %all-gather.3.cloned.1.call-update) | async-done | bytes 10485776 | tf_op jit(solution)/shard_map/all_gather | solution.py:28
  102.8 13.8 %copy.58 = bf16[256,20480]{0,1:T(8,128)(2,1)} copy(bf16[256,20480]{1,0:T(8,128)(2,1)} %all-gather.3.cloned.1.call-done) | data formatting | bytes 20971520 | tf_op jit(solution)/shard_map/all_gather | solution.py:28
  116.5 14.4 %copy.60 = bf16[256,80,256]{2,0,1:T(8,128)(2,1)} copy(bf16[256,80,256]{0,2,1:T(8,128)(2,1)} %bitcast.50) | data formatting | bytes 20971520 | tf_op jit(solution)/shard_map/reshape | solution.py:30
  130.9 6.8 %gather_fusion = bf16[32,256,256]{2,1,0:T(8,128)(2,1)} fusion(bf16[256,80,256]{2,0,1:T(8,128)(2,1)} %copy.60, s32[1024]{0:T(1024)S(1)} %pad_clamp_fusion.1), kind=kCustom, calls=%fused_computation | custom fusion | bytes 8388736 | tf_op jit(solution)/shard_map/jit(_take)/gather | solution.py:32
  137.7 6.2 %copy.61 = bf16[256,4,8,256]{0,3,2,1:T(8,128)(2,1)} copy(bf16[256,4,8,256]{3,0,2,1:T(8,128)(2,1)} %bitcast.52) | data formatting | bytes 8388608 | tf_op jit(solution)/shard_map/jit(_take)/gather | solution.py:32
  144.0 6.2 %fusion = f32[4,256,256,1]{2,1,3,0:T(8,128)} fusion(bf16[4,8,256,256]{3,2,1,0:T(8,128)(2,1)} %param.13, bf16[256,4,8,256]{0,3,2,1:T(8,128)(2,1)} %copy.61, pred[4,8]{1,0:T(4,128)(4,1)S(1)} %copy.57, bf16[4,8]{1,0:T(4,128)(2,1)S(1)} %get-tuple-element.19), kind=kOutput, calls=%fused_computation.4 | convolution fusion | flops 1077936128 | bytes 9437280 | tf_op jit(solution)/shard_map/frkb,rkbo->fro/dot_general | solution.py:35
  150.3 37.7 %reduce-scatter.4.cloned.1.call-done = f32[256,128]{0,1:T(8,128)} async-done(((f32[256,1024]{0,1:T(8,128)}), f32[256,128]{0,1:T(8,128)}) %reduce-scatter.4.cloned.1.call-update) | async-done | bytes 131088 | tf_op jit(solution)/shard_map/reduce_scatter | solution.py:38
  188.0 1.6 tanh_convert_fusion.1
  189.9 56.9 %all-gather.5.cloned.1.call-done = bf16[256,4096]{0,1:T(8,128)(2,1)} async-done(((bf16[256,128]{0,1:T(8,128)(2,1)}), bf16[256,4096]{0,1:T(8,128)(2,1)}) %all-gather.5.cloned.1.call-update) | async-done | bytes 2097168 | tf_op jit(solution)/shard_map/all_gather | solution.py:40
  246.8 2.8 copy.64
  249.6 2.0 gather_fusion.1
  251.6 4.3 copy.65
  256.0 3.6 fusion.8
  259.9 36.5 %reduce-scatter.6.cloned.1.call-done = f32[256,128]{0,1:T(8,128)} async-done(((f32[256,1024]{0,1:T(8,128)}), f32[256,128]{0,1:T(8,128)}) %reduce-scatter.6.cloned.1.call-update) | async-done | bytes 131088 | tf_op jit(solution)/shard_map/reduce_scatter | solution.py:48
  296.4 1.0 multiply_convert_fusion.3
  297.4 28.9 %all_gather.14 = bf16[256,1024]{0,1:T(8,128)(2,1)S(1)} all-gather(bf16[256,128]{0,1:T(8,128)(2,1)S(1)} %get-tuple-element.12), channel_id=1, replica_groups=mesh['out'=32,'in'=8] {'in'}, dimensions={1}, use_global_device_ids=true | all-gather | bytes 589824 | tf_op jit(solution)/shard_map/all_gather | solution.py:52
  326.2 2.8 fusion.6
  329.0 5.5 %copy.70 = f32[256,16,256]{2,1,0:T(8,128)} copy(f32[256,16,256]{0,2,1:T(8,128)} %bitcast.51) | data formatting | bytes 8388608 | tf_op jit(solution)/shard_map/reshape | solution.py:61
  334.5 4.3 convert_bitcast_fusion
  338.9 2.7 copy.86
  342.4 3.7 multiply_convert_fusion.1
  346.0 88.3 %reduce-scatter.8.cloned.1.call-done = bf16[256,128]{0,1:T(8,128)(2,1)} async-done(((bf16[256,4096]{0,1:T(8,128)(2,1)}), bf16[256,128]{0,1:T(8,128)(2,1)}) %reduce-scatter.8.cloned.1.call-update) | async-done | bytes 65552 | tf_op jit(solution)/shard_map/reduce_scatter | solution.py:69
  435.2 29.0 %all_gather.15 = bf16[256,1024]{0,1:T(8,128)(2,1)S(1)} all-gather(bf16[256,128]{0,1:T(8,128)(2,1)S(1)} %multiply_convert_fusion.2), channel_id=1, replica_groups=mesh['out'=32,'in'=8] {'in'}, dimensions={1}, use_global_device_ids=true | all-gather | bytes 589824 | tf_op jit(solution)/shard_map/all_gather | solution.py:74
  464.2 5.5 %multiply_convert_fusion = bf16[4,8,256,256]{3,2,1,0:T(8,128)(2,1)} fusion(f32[4,8]{1,0:T(4,128)S(1)} %get-tuple-element.18, bf16[256,4,256,1]{0,2,3,1:T(8,128)(2,1)S(1)} %bitcast.60, bf16[256,4,8,256]{0,3,2,1:T(8,128)(2,1)} %copy.61, pred[4,8]{1,0:T(4,128)(4,1)S(1)} %copy.57), kind=kOutput, calls=%fused_computation.2 | convolution fusion | flops 1080033280 | bytes 8913056 | tf_op jit(solution)/shard_map/frkb,fro->rkbo/dot_general | solution.py:75
  (39 shorter events, 4.8 us)
Async XLA Ops:
  7.2 95.6 %all-gather.3.cloned.1.call-start = ((), (), s32[]{:S(2)}) async-start(), calls=%async_computation.3 | async-start | bytes 10813440 | tf_op jit(solution)/shard_map/all_gather | solution.py:28
  7.9 180.1 %reduce-scatter.4.cloned.1.call-start = ((), (), s32[]{:S(2)}) async-start(), calls=%async_computation.4 | async-start | bytes 1179648 | tf_op jit(solution)/shard_map/reduce_scatter | solution.py:38
  144.0 44.0 %copy-start.4 = (f32[128]{0:T(128)S(1)}, f32[128]{0:T(128)}, u32[]{:S(2)}) copy-start(f32[128]{0:T(128)} %param.14) | copy-start | bytes 1540
  144.0 45.7 %copy-start.3 = (s32[4,4]{1,0:T(4,128)S(1)}, s32[4,4]{1,0:T(4,128)}, u32[]{:S(2)}) copy-start(s32[4,4]{1,0:T(4,128)} %param.15) | copy-start | bytes 196
  144.0 45.8 %copy-start.6 = (s32[4,1]{0,1:T(1,128)S(1)}, s32[4,1]{0,1:T(1,128)}, u32[]{:S(2)}) copy-start(s32[4,1]{0,1:T(1,128)} %param.16) | copy-start | bytes 52
  150.2 96.5 %all-gather.5.cloned.1.call-start = ((), (), s32[]{:S(2)}) async-start(), calls=%async_computation.5 | async-start | bytes 2162688 | tf_op jit(solution)/shard_map/all_gather | solution.py:40
  189.6 106.7 %reduce-scatter.6.cloned.1.call-start = ((), (), s32[]{:S(2)}) async-start(), calls=%async_computation.6 | async-start | bytes 1179648 | tf_op jit(solution)/shard_map/reduce_scatter | solution.py:48
  251.6 4.3 copy-start
  256.0 3.8 copy-start.2
  256.0 40.4 %copy-start.5 = (f32[128]{0:T(128)S(1)}, f32[128]{0:T(128)}, u32[]{:S(2)}) copy-start(f32[128]{0:T(128)} %param.18) | copy-start | bytes 1540
  259.6 174.7 %reduce-scatter.8.cloned.1.call-start = ((), (), s32[]{:S(2)}) async-start(), calls=%async_computation.7 | async-start | bytes 2162688 | tf_op jit(solution)/shard_map/reduce_scatter | solution.py:69
  341.6 92.7 %copy-start.1 = (f32[256,128]{0,1:T(8,128)S(1)}, f32[256,128]{0,1:T(8,128)}, u32[]{:S(2)}) copy-start(f32[256,128]{0,1:T(8,128)} %reduce-scatter.4.cloned.1.call-done) | copy-start | bytes 393220
Sparse Core Ops, SparseCore 0:
  10.5 92.1 all-gather.2
  150.4 37.5 reduce-scatter.3
  191.1 55.6 all-gather.4
  259.7 36.5 reduce-scatter.5
  341.7 92.4 reduce-scatter.7
where the time goes:
time: 478 us; the launch traced here: 476 us
  waiting for transfers between devices  313 us (65%)
  local copies, waits for them, and re-layouts  59.9 us (13%)
  blocking collectives  57.9 us (12%)
  matrix products  26.1 us (5%)
  between operations  13.9 us (3%)
  other arithmetic  5.16 us (1%)
    all_gather x1, waiting for transfers between devices, shards(): gathered = lax.all_gather(slopes, 'out', axis=0, tiled=True)  93.1 us
    reduce_scatter x1, waiting for transfers between devices, shards(): lax.psum_scatter(spread.astype(jnp.bfloat16), 'out', scatter_dimension=1,...  88.3 us
    all_gather x1, waiting for transfers between devices, shards(): second_input = lax.all_gather(hidden_first, 'out', axis=1, tiled=True)  56.9 us
    reduce_scatter x1, waiting for transfers between devices, shards(): lax.psum_scatter(partial_first, 'in', scatter_dimension=1, tiled=True)  37.7 us
    reduce_scatter x1, waiting for transfers between devices, shards(): lax.psum_scatter(partial_second, 'in', scatter_dimension=1, tiled=True)  36.5 us
    all_gather x1, blocking collectives, shards(): lax.all_gather(delta_first, 'in', axis=1, tiled=True)  29 us
    all_gather x1, blocking collectives, shards(): lax.all_gather(delta_second, 'in', axis=1, tiled=True)  28.9 us
    reshape x1, local copies, waits for them, and re-layouts, shards(): slope_blocks = gathered.reshape(frames, -1, BLK)  14.4 us
  transfers between devices with their start and end apart: 5, of which 5 were waited for; matrix products, arithmetic and copies ran while one was open for 1% of the time, Pallas kernels for 0%

commit v1 on v0

--- a/solution.py
+++ b/solution.py
@@ -2,6 +2,7 @@
 import jax.numpy as jnp
 from jax import lax
 from jax.sharding import PartitionSpec as P
+from jax.lax import all_to_all, axis_size
 
 BLK = 256
 KD1 = 8
@@ -25,7 +26,13 @@
     live_second = jnp.arange(KD2, dtype=jnp.int32)[None, :] < count_second
     masked_first = weight_first * live_first.astype(jnp.bfloat16)[:, :, None, None]
     masked_second = weight_second * live_second.astype(jnp.bfloat16)[:, :, None, None]
-    gathered = lax.all_gather(slopes, "out", axis=0, tiled=True)
+    tell_stocks = lambda load: jnp.concatenate(
+        all_to_all(
+            jnp.stack([load for _ in range(axis_size("out"))]), "out", split_axis=0, concat_axis=0
+        ),
+        axis=0,
+    )
+    gathered = tell_stocks(slopes)
     frames = gathered.shape[0]
     slope_blocks = gathered.reshape(frames, -1, BLK)
     own_cols = lax.dynamic_slice_in_dim(cols_first, lax.axis_index("out") * rows, rows, 0)

time: 478 us -> 624 us (1.31)
  waiting for transfers between devices: 313 us -> 448 us
  starting transfers between devices: 0.2 us -> 11.9 us
    all_to_all x0 -> x1, waiting for transfers between devices: none -> 232 us  [shards(): all_to_all(jnp.stack([load for _ in range(axis_size('out'))]), 'out', spl...]
    all_gather x1 -> x0, waiting for transfers between devices: 93.1 us -> none  [shards(): gathered = lax.all_gather(slopes, 'out', axis=0, tiled=True)]
    another operation x0 -> x2, local copies, waits for them, and re-layouts: none -> 17.8 us  [the longest x1 11.8 us: shards(): slope_blocks = gathered.reshape(frames, -1, BLK)]
    reshape x1 -> x0, local copies, waits for them, and re-layouts: 14.4 us -> none  [shards(): slope_blocks = gathered.reshape(frames, -1, BLK)]
    all_gather x1 -> x0, local copies, waits for them, and re-layouts: 13.8 us -> none  [shards(): gathered = lax.all_gather(slopes, 'out', axis=0, tiled=True)]
    all_to_all x0 -> x1, starting transfers between devices: none -> 11.6 us  [shards(): all_to_all(jnp.stack([load for _ in range(axis_size('out'))]), 'out', spl...]
    unnamed x16 -> x21, local copies, waits for them, and re-layouts: 0.87 us -> 12 us
where the time goes in v1:
time: 624 us; the launch traced here: 623 us
  waiting for transfers between devices  448 us (72%)
  local copies, waits for them, and re-layouts  60.7 us (10%)
  blocking collectives  57.9 us (9%)
  matrix products  26.1 us (4%)
  between operations  13.9 us (2%)
  starting transfers between devices  11.9 us (2%)
    all_to_all x1, waiting for transfers between devices, shards(): all_to_all(jnp.stack([load for _ in range(axis_size('out'))]), 'out', spl...  232 us
    reduce_scatter x1, waiting for transfers between devices, shards(): lax.psum_scatter(spread.astype(jnp.bfloat16), 'out', scatter_dimension=1,...  88.4 us
    all_gather x1, waiting for transfers between devices, shards(): second_input = lax.all_gather(hidden_first, 'out', axis=1, tiled=True)  56.7 us
    reduce_scatter x1, waiting for transfers between devices, shards(): lax.psum_scatter(partial_second, 'in', scatter_dimension=1, tiled=True)  36.5 us
    reduce_scatter x1, waiting for transfers between devices, shards(): lax.psum_scatter(partial_first, 'in', scatter_dimension=1, tiled=True)  34.5 us
    all_gather x1, blocking collectives, shards(): lax.all_gather(delta_first, 'in', axis=1, tiled=True)  29 us
    all_gather x1, blocking collectives, shards(): lax.all_gather(delta_second, 'in', axis=1, tiled=True)  28.9 us
    gather x2, local copies, waits for them, and re-layouts, shards(): jnp.take(slope_blocks, own_cols.reshape(-1), axis=1)  13 us
  transfers between devices with their start and end apart: 5, of which 5 were waited for; matrix products, arithmetic and copies ran while one was open for 1% of the time, Pallas kernels for 0%

profile of v1, /device:TPU:24, one launch (start us, length us, event | category | flops | bytes accessed | tf_op | source)
XLA Modules:
  0.0 622.7 jit_solution(613765203094674321)
XLA Ops:
  7.2 6.0 stack.2
  13.2 11.6 %all-to-all-start = ((bf16[32,8,20480]{2,1,0:T(8,128)(2,1)}), bf16[32,8,20480]{2,1,0:T(8,128)(2,1)}, u32[]{:S(2)}, u32[]{:S(2)}) async-start(bf16[32,8,20480]{2,1,0:T(8,128)(2,1)} %stack.2), calls=%async_computation | async-start | bytes 20971520 | tf_op jit(solution)/shard_map/all_to_all | solution.py:30
  25.2 232.3 %all-to-all-done = bf16[32,8,20480]{2,1,0:T(8,128)(2,1)} async-done(((bf16[32,8,20480]{2,1,0:T(8,128)(2,1)}), bf16[32,8,20480]{2,1,0:T(8,128)(2,1)}, u32[]{:S(2)}, u32[]{:S(2)}) %all-to-all-start) | async-done | bytes 10485792 | tf_op jit(solution)/shard_map/all_to_all | solution.py:30
  257.6 11.2 %copy.71 = bf16[32,8,80,256]{3,2,1,0:T(8,128)(2,1)} copy(bf16[32,8,80,256]{3,1,2,0:T(8,128)(2,1)} %bitcast.41) | data formatting | bytes 20971520
  268.7 11.8 %copy.40 = bf16[256,80,256]{2,0,1:T(8,128)(2,1)} copy(bf16[256,80,256]{2,1,0:T(8,128)(2,1)} %bitcast.52) | data formatting | bytes 20971520 | tf_op jit(solution)/shard_map/reshape;reshape | solution.py:37
  280.5 6.8 %gather_fusion = bf16[32,256,256]{2,1,0:T(8,128)(2,1)} fusion(bf16[256,80,256]{2,0,1:T(8,128)(2,1)} %copy.40, s32[1024]{0:T(1024)S(1)} %pad_clamp_fusion.1), kind=kCustom, calls=%fused_computation | custom fusion | bytes 8388736 | tf_op jit(solution)/shard_map/jit(_take)/gather | solution.py:39
  287.3 6.2 copy.41
  293.5 6.2 %fusion = f32[4,256,256,1]{2,1,3,0:T(8,128)} fusion(bf16[4,8,256,256]{3,2,1,0:T(8,128)(2,1)} %param.13, bf16[256,4,8,256]{0,3,2,1:T(8,128)(2,1)} %copy.41, pred[4,8]{1,0:T(4,128)(4,1)S(1)} %copy.38, bf16[4,8]{1,0:T(4,128)(2,1)S(1)} %get-tuple-element.16), kind=kOutput, calls=%fused_computation.4 | convolution fusion | flops 1077936128 | bytes 9437280 | tf_op jit(solution)/shard_map/frkb,rkbo->fro/dot_general | solution.py:42
  299.8 34.5 %reduce-scatter.4.cloned.1.call-done = f32[256,128]{0,1:T(8,128)} async-done(((f32[256,1024]{0,1:T(8,128)}), f32[256,128]{0,1:T(8,128)}) %reduce-scatter.4.cloned.1.call-update) | async-done | bytes 131088 | tf_op jit(solution)/shard_map/reduce_scatter | solution.py:45
  336.4 56.7 %all-gather.2.cloned.1.call-done = bf16[256,4096]{0,1:T(8,128)(2,1)} async-done(((bf16[256,128]{0,1:T(8,128)(2,1)}), bf16[256,4096]{0,1:T(8,128)(2,1)}) %all-gather.2.cloned.1.call-update) | async-done | bytes 2097168 | tf_op jit(solution)/shard_map/all_gather | solution.py:47
  393.1 2.8 copy.44
  395.9 2.0 gather_fusion.1
  397.9 4.3 copy.45
  402.3 3.6 fusion.8
  406.1 36.5 %reduce-scatter.6.cloned.1.call-done = f32[256,128]{0,1:T(8,128)} async-done(((f32[256,1024]{0,1:T(8,128)}), f32[256,128]{0,1:T(8,128)}) %reduce-scatter.6.cloned.1.call-update) | async-done | bytes 131088 | tf_op jit(solution)/shard_map/reduce_scatter | solution.py:55
  443.7 28.9 %all_gather.10 = bf16[256,1024]{0,1:T(8,128)(2,1)S(1)} all-gather(bf16[256,128]{0,1:T(8,128)(2,1)S(1)} %get-tuple-element.9), channel_id=1, replica_groups=mesh['out'=32,'in'=8] {'in'}, dimensions={1}, use_global_device_ids=true | all-gather | bytes 589824 | tf_op jit(solution)/shard_map/all_gather | solution.py:59
  472.5 2.8 fusion.6
  475.3 5.5 copy.50
  480.8 4.3 convert_bitcast_fusion
  485.1 2.7 copy.66
  488.6 3.7 multiply_convert_fusion.1
  492.3 88.4 %reduce-scatter.8.cloned.1.call-done = bf16[256,128]{0,1:T(8,128)(2,1)} async-done(((bf16[256,4096]{0,1:T(8,128)(2,1)}), bf16[256,128]{0,1:T(8,128)(2,1)}) %reduce-scatter.8.cloned.1.call-update) | async-done | bytes 65552 | tf_op jit(solution)/shard_map/reduce_scatter | solution.py:76
  581.6 29.0 %all_gather.11 = bf16[256,1024]{0,1:T(8,128)(2,1)S(1)} all-gather(bf16[256,128]{0,1:T(8,128)(2,1)S(1)} %multiply_convert_fusion.2), channel_id=1, replica_groups=mesh['out'=32,'in'=8] {'in'}, dimensions={1}, use_global_device_ids=true | all-gather | bytes 589824 | tf_op jit(solution)/shard_map/all_gather | solution.py:81
  610.6 5.5 multiply_convert_fusion
  (43 shorter events, 5.5 us)
Async XLA Ops:
  13.1 11.6 %copy-start.4 = (s32[128,8]{0,1:T(8,128)S(1)}, s32[128,8]{0,1:T(8,128)}, u32[]{:S(2)}) copy-start(s32[128,8]{0,1:T(8,128)} %param.11) | copy-start | bytes 12292
  13.1 12.0 %copy-start.7 = (s32[4,1]{0,1:T(1,128)S(1)}, s32[4,1]{0,1:T(1,128)}, u32[]{:S(2)}) copy-start(s32[4,1]{0,1:T(1,128)} %param.12) | copy-start | bytes 52
  13.2 244.4 %all-to-all-start = ((bf16[32,8,20480]{2,1,0:T(8,128)(2,1)}), bf16[32,8,20480]{2,1,0:T(8,128)(2,1)}, u32[]{:S(2)}, u32[]{:S(2)}) async-start(bf16[32,8,20480]{2,1,0:T(8,128)(2,1)} %stack.2), calls=%async_computation | async-start | bytes 20971520 | tf_op jit(solution)/shard_map/all_to_all | solution.py:30
  24.7 309.6 %reduce-scatter.4.cloned.1.call-start = ((), (), s32[]{:S(2)}) async-start(), calls=%async_computation.4 | async-start | bytes 1179648 | tf_op jit(solution)/shard_map/reduce_scatter | solution.py:45
  293.5 40.8 %copy-start.5 = (f32[128]{0:T(128)S(1)}, f32[128]{0:T(128)}, u32[]{:S(2)}) copy-start(f32[128]{0:T(128)} %param.14) | copy-start | bytes 1540
  293.5 42.7 %copy-start.3 = (s32[4,4]{1,0:T(4,128)S(1)}, s32[4,4]{1,0:T(4,128)}, u32[]{:S(2)}) copy-start(s32[4,4]{1,0:T(4,128)} %param.15) | copy-start | bytes 196
  293.5 42.8 %copy-start.8 = (s32[4,1]{0,1:T(1,128)S(1)}, s32[4,1]{0,1:T(1,128)}, u32[]{:S(2)}) copy-start(s32[4,1]{0,1:T(1,128)} %param.16) | copy-start | bytes 52
  299.8 93.3 %all-gather.2.cloned.1.call-start = ((), (), s32[]{:S(2)}) async-start(), calls=%async_computation.5 | async-start | bytes 2162688 | tf_op jit(solution)/shard_map/all_gather | solution.py:47
  336.0 106.7 %reduce-scatter.6.cloned.1.call-start = ((), (), s32[]{:S(2)}) async-start(), calls=%async_computation.6 | async-start | bytes 1179648 | tf_op jit(solution)/shard_map/reduce_scatter | solution.py:55
  397.9 4.3 copy-start
  402.3 3.8 copy-start.2
  402.3 40.4 %copy-start.6 = (f32[128]{0:T(128)S(1)}, f32[128]{0:T(128)}, u32[]{:S(2)}) copy-start(f32[128]{0:T(128)} %param.18) | copy-start | bytes 1540
  405.9 174.8 %reduce-scatter.8.cloned.1.call-start = ((), (), s32[]{:S(2)}) async-start(), calls=%async_computation.7 | async-start | bytes 2162688 | tf_op jit(solution)/shard_map/reduce_scatter | solution.py:76
  487.9 92.8 %copy-start.1 = (f32[256,128]{0,1:T(8,128)S(1)}, f32[256,128]{0,1:T(8,128)}, u32[]{:S(2)}) copy-start(f32[256,128]{0,1:T(8,128)} %reduce-scatter.4.cloned.1.call-done) | copy-start | bytes 393220
Sparse Core Ops, SparseCore 0:
  299.9 34.3 reduce-scatter.3
  337.5 55.5 all-gather.1
  406.0 36.5 reduce-scatter.5
  488.0 92.6 reduce-scatter.7
